TPU v7x, 32 devices: a whole 2x2x4 slice. The times are simulated.
32 devices in a mesh: kpt: 2 (over core), orb: 16 (over z, y, x).
Axes of the slice: x: 2, y: 2, z: 4, core: 2. Of those that a mesh axis runs over, the one named last changes fastest.
Arguments:
- orbitals: bfloat16 [2, 512, 64, 1024], P('kpt', 'orb'), may hold values from -6 to 6
- potential: float32 [64, 1024], replicated, may hold values from 0.5 to 12
Outputs:
- rotated: bfloat16 [2, 512, 64, 1024], P('kpt', 'orb')
- density: float32 [64, 1024], P('orb')
All inputs are finite; a program needn't handle non-finite values.
Results may differ from a plain program's by a relative error of at most 0.0068.
The roundings to bfloat16 on the way count: a program that leaves them out, or rounds other values in their place, can miss the bound.
Values may be sent and summed in bfloat16 or wider, within the bound.
No kernel may reach another device: no remote copies, remote signals or barrier semaphores. Data moves between devices by JAX's collectives and lax.ppermute only.
A program may use at most 128 MiB of HBM per device.

v0:
```python
import math
import jax
import jax.numpy as jnp
import numpy as np
from jax import lax
from jax.sharding import PartitionSpec as P

NX = 64
NY = 32
NZ = 32
DEG = 4
ITERS = 8
filter_centre = 13.0
filter_half = 9.0
margin_eps = 1e-06


def circulant(taps, first, length):
    matrix = np.zeros((length, length))
    for k in range(len(taps)):
        for i in range(length):
            matrix[i, (i + first + k) % length] += taps[k]
    return matrix


def build_tables(size_x, size_y, size_z):
    kinetic = [math.pi**2 / 6.0 if k == 0 else (-1.0) ** k / (k * k) for k in range(-14, 15)]
    smooth_taps = np.array([math.exp(-((k + 0.5) ** 2) / 6.0) for k in range(-8, 8)])
    smooth_taps = smooth_taps / smooth_taps.sum()
    kin_x = circulant(kinetic, -14, size_x)
    mag_x = circulant(smooth_taps, -8, size_x)
    kin_yz = np.kron(circulant(kinetic, -14, size_y), np.eye(size_z)) + np.kron(
        np.eye(size_y), circulant(kinetic, -14, size_z)
    )
    mag_yz = np.kron(circulant(smooth_taps, -8, size_y), circulant(smooth_taps, -8, size_z))
    yz_table = np.concatenate([kin_yz.T, mag_yz.T], axis=1)
    result = [kin_x, mag_x, mag_x.T, yz_table, mag_yz]
    return [jnp.asarray(table, jnp.float32).astype(jnp.bfloat16) for table in result]


def hamiltonian(block, potential, tables):
    kin_x, mag_x, mag_xt, yz_table, mag_yz = tables
    width = block.shape[2]
    both = jnp.einsum("bxc,cd->bxd", block, yz_table, preferred_element_type=jnp.float32)
    smooth = both[:, :, width:].astype(jnp.bfloat16)
    kin_all = (
        jnp.einsum("ux,bxc->buc", kin_x, block, preferred_element_type=jnp.float32)
        + both[:, :, :width]
    )
    weighted = (
        potential[None]
        * jnp.einsum("ux,bxc->buc", mag_x, smooth, preferred_element_type=jnp.float32)
    ).astype(jnp.bfloat16)
    back = jnp.einsum("ux,bxc->buc", mag_xt, weighted, preferred_element_type=jnp.float32).astype(
        jnp.bfloat16
    )
    return kin_all + jnp.einsum("bxc,cd->bxd", back, mag_yz, preferred_element_type=jnp.float32)


def chebyshev(block, potential, tables):
    prev = block
    shifted = hamiltonian(block, potential, tables) - filter_centre * block.astype(jnp.float32)
    now = (shifted / filter_half).astype(jnp.bfloat16)
    for step in range(DEG - 1):
        shifted = hamiltonian(now, potential, tables) - filter_centre * now.astype(jnp.float32)
        nxt = (2.0 * shifted / filter_half - prev.astype(jnp.float32)).astype(jnp.bfloat16)
        prev, now = (now, nxt)
    return now


def shards(orbitals, potential):
    width = orbitals.shape[3]
    tables = build_tables(NX, NY, NZ)
    hp = lax.Precision.HIGHEST
    filtered = chebyshev(orbitals[0], potential, tables)[None]
    spread = lax.all_to_all(filtered, "orb", split_axis=2, concat_axis=1, tiled=True)
    count_orb = spread.shape[1]
    rows_dev = spread.shape[2]
    cells = NX * NY * NZ
    flat = spread[0].reshape(count_orb, rows_dev * width)
    inverse_cells = 1.0 / cells
    partial_margin = (
        lax.dot_general(flat, flat, (((1,), (1,)), ((), ())), preferred_element_type=jnp.float32)
        * inverse_cells
    )
    margin = lax.psum(partial_margin, "orb")
    scale = jnp.sqrt(jnp.sum(margin * margin) + margin_eps)
    eye = jnp.eye(count_orb, dtype=jnp.float32)
    iterate_a = margin / scale
    iterate_z = eye
    for step in range(ITERS):
        factor = 0.5 * (3.0 * eye - jnp.dot(iterate_z, iterate_a, precision=hp))
        iterate_a = jnp.dot(factor, iterate_a, precision=hp)
        iterate_z = jnp.dot(factor, iterate_z, precision=hp)
    coeff = (iterate_z / jnp.sqrt(scale)).astype(jnp.bfloat16)
    rotated_flat = lax.dot_general(
        coeff, flat, (((0,), (0,)), ((), ())), preferred_element_type=jnp.float32
    ).astype(jnp.bfloat16)
    rotated_cells = rotated_flat.reshape(1, count_orb, rows_dev, width)
    rotated = lax.all_to_all(rotated_cells, "orb", split_axis=1, concat_axis=2, tiled=True)
    weight = 1.0 / (lax.axis_size("kpt") * math.sqrt(count_orb))
    values = rotated_flat.astype(jnp.float32)
    own_density = (jnp.sum(values * values, axis=0) * weight).reshape(rows_dev, width)
    density = lax.psum(own_density, "kpt")
    return (rotated, density)


def solution(mesh):
    in_specs = (P("kpt", "orb", None, None), P())
    out_specs = (P("kpt", "orb", None, None), P("orb", None))
    return jax.shard_map(shards, mesh=mesh, in_specs=in_specs, out_specs=out_specs, check_vma=False)
```

profile of v0, /device:TPU:14, one launch (start us, length us, event | category | flops | bytes accessed | tf_op | source)
XLA Modules:
  0.0 567.5 jit_solution(11716203920185398709)
XLA Ops:
  7.2 15.1 %convolution_bitcast_fusion = f32[32,64,2048]{2,1,0:T(8,128)} fusion(bf16[1024,2048,1]{1,0,2:T(8,128)(2,1)} %constant.48, bf16[1,32,64,1024]{3,2,1,0:T(8,128)(2,1)} %param.7), kind=kOutput, calls=%fused_computation.39 | convolution fusion | flops 8589934592 | bytes 25165824 | tf_op jit(solution)/shard_map/bxc,cd->bxd/dot_general | solution.py:44
  22.4 7.7 %fusion.20 = bf16[32,1024,64]{1,2,0:T(8,128)(2,1)} fusion(bf16[64,64,1]{1,0,2:T(8,128)(2,1)S(1)} %copy-done.14, f32[64,1024]{1,0:T(8,128)S(1)} %copy-done.10, bf16[64,64,1]{1,0,2:T(8,128)(2,1)S(1)} %copy-done.15, f32[32,64,2048]{2,1,0:T(8,128)} %convolution_bitcast_fusion), kind=kOutput, calls=%fused_computation.41 | convolution fusion | flops 541065216 | bytes 8667136 | tf_op jit(solution)/shard_map/ux,bxc->buc/dot_general | solution.py:54
  30.1 7.1 %fusion.39 = f32[32,64,1024]{2,1,0:T(8,128)S(1)} fusion(bf16[1024,1024,1]{1,0,2:T(8,128)(2,1)} %constant.51, bf16[32,1024,64]{1,2,0:T(8,128)(2,1)} %fusion.20), kind=kOutput, calls=%fused_computation.56 | convolution fusion | flops 4294967296 | bytes 14680064 | tf_op jit(solution)/shard_map/bxc,cd->bxd/dot_general | solution.py:57
  37.2 5.4 fusion.2
  44.6 14.5 %fusion.65 = f32[32,64,2048]{2,1,0:T(8,128)} fusion(bf16[32,64,1024]{2,1,0:T(8,128)(2,1)S(1)} %fusion.2, bf16[1024,2048,1]{1,0,2:T(8,128)(2,1)} %constant.48), kind=kOutput, calls=%fused_computation.94 | convolution fusion | flops 8589934592 | bytes 25165824 | tf_op jit(solution)/shard_map/bxc,cd->bxd/dot_general | solution.py:44
  59.1 7.7 %fusion.22 = bf16[32,1024,64]{1,2,0:T(8,128)(2,1)} fusion(bf16[64,64,1]{1,0,2:T(8,128)(2,1)S(1)} %copy-done.14, f32[64,1024]{1,0:T(8,128)S(1)} %copy-done.10, bf16[64,64,1]{1,0,2:T(8,128)(2,1)S(1)} %copy-done.15, f32[32,64,2048]{2,1,0:T(8,128)} %fusion.65), kind=kOutput, calls=%fused_computation.42 | convolution fusion | flops 541065216 | bytes 8667136 | tf_op jit(solution)/shard_map/ux,bxc->buc/dot_general | solution.py:54
  66.8 10.8 %fusion.37 = f32[32,64,1024]{2,1,0:T(8,128)} fusion(bf16[1024,1024,1]{1,0,2:T(8,128)(2,1)} %constant.51, bf16[32,1024,64]{1,2,0:T(8,128)(2,1)} %fusion.22), kind=kOutput, calls=%fused_computation.54 | convolution fusion | flops 4294967296 | bytes 14680064 | tf_op jit(solution)/shard_map/bxc,cd->bxd/dot_general | solution.py:57
  77.5 7.6 %fusion.3 = bf16[32,64,1024]{2,1,0:T(8,128)(2,1)S(1)} fusion(bf16[32,64,1024]{2,1,0:T(8,128)(2,1)S(1)} %copy-done.4, f32[32,64,1024]{2,1,0:T(8,128)} %fusion.37, f32[32,64,2048]{2,1,0:T(8,128)} %fusion.65, bf16[1,32,64,1024]{3,2,1,0:T(8,128)(2,1)S(1)} %copy-done.9, bf16[64,64,1]{1,0,2:T(8,128)(2,1)S(1)} %copy-done.16), kind=kOutput, calls=%fused_computation.9 | convolution fusion | flops 287309824 | bytes 33570816 | tf_op jit(solution)/shard_map/ux,bxc->buc/dot_general | solution.py:47
  87.1 14.0 %fusion.66 = f32[32,64,2048]{2,1,0:T(8,128)} fusion(bf16[32,64,1024]{2,1,0:T(8,128)(2,1)S(1)} %fusion.3, bf16[1024,2048,1]{1,0,2:T(8,128)(2,1)} %constant.48), kind=kOutput, calls=%fused_computation.95 | convolution fusion | flops 8589934592 | bytes 25165824 | tf_op jit(solution)/shard_map/bxc,cd->bxd/dot_general | solution.py:44
  101.1 7.8 %fusion.24 = bf16[32,1024,64]{1,2,0:T(8,128)(2,1)} fusion(bf16[64,64,1]{1,0,2:T(8,128)(2,1)S(1)} %copy-done.14, f32[64,1024]{1,0:T(8,128)S(1)} %copy-done.10, bf16[64,64,1]{1,0,2:T(8,128)(2,1)S(1)} %copy-done.15, f32[32,64,2048]{2,1,0:T(8,128)} %fusion.66), kind=kOutput, calls=%fused_computation.43 | convolution fusion | flops 541065216 | bytes 8667136 | tf_op jit(solution)/shard_map/ux,bxc->buc/dot_general | solution.py:54
  108.9 9.2 %fusion.35 = f32[32,64,1024]{2,1,0:T(8,128)} fusion(bf16[1024,1024,1]{1,0,2:T(8,128)(2,1)S(1)} %copy-done.17, bf16[32,1024,64]{1,2,0:T(8,128)(2,1)} %fusion.24), kind=kOutput, calls=%fused_computation.52 | convolution fusion | flops 4294967296 | bytes 14680064 | tf_op jit(solution)/shard_map/bxc,cd->bxd/dot_general | solution.py:57
  118.1 7.6 %fusion.6 = bf16[32,64,1024]{2,1,0:T(8,128)(2,1)S(1)} fusion(bf16[32,64,1024]{2,1,0:T(8,128)(2,1)S(1)} %copy-done.5, bf16[32,64,1024]{2,1,0:T(8,128)(2,1)S(1)} %copy-done.1, f32[32,64,1024]{2,1,0:T(8,128)} %fusion.35, f32[32,64,2048]{2,1,0:T(8,128)} %fusion.66, bf16[64,64,1]{1,0,2:T(8,128)(2,1)S(1)} %copy-done.16), kind=kOutput, calls=%fused_computation.12 | convolution fusion | flops 287309824 | bytes 33570816 | tf_op jit(solution)/shard_map/ux,bxc->buc/dot_general | solution.py:47
  127.8 14.1 %fusion.67 = f32[32,64,2048]{2,1,0:T(8,128)} fusion(bf16[32,64,1024]{2,1,0:T(8,128)(2,1)S(1)} %fusion.6, bf16[1024,2048,1]{1,0,2:T(8,128)(2,1)} %constant.48), kind=kOutput, calls=%fused_computation.96 | convolution fusion | flops 8589934592 | bytes 25165824 | tf_op jit(solution)/shard_map/bxc,cd->bxd/dot_general | solution.py:44
  141.8 7.8 %fusion.26 = bf16[32,1024,64]{1,2,0:T(8,128)(2,1)} fusion(bf16[64,64,1]{1,0,2:T(8,128)(2,1)S(1)} %copy-done.14, f32[64,1024]{1,0:T(8,128)S(1)} %copy-done.10, bf16[64,64,1]{1,0,2:T(8,128)(2,1)S(1)} %copy-done.15, f32[32,64,2048]{2,1,0:T(8,128)} %fusion.67), kind=kOutput, calls=%fused_computation.44 | convolution fusion | flops 541065216 | bytes 8667136 | tf_op jit(solution)/shard_map/ux,bxc->buc/dot_general | solution.py:54
  149.6 9.2 %fusion.33 = f32[32,64,1024]{2,1,0:T(8,128)} fusion(bf16[1024,1024,1]{1,0,2:T(8,128)(2,1)S(1)} %copy-done.18, bf16[32,1024,64]{1,2,0:T(8,128)(2,1)} %fusion.26), kind=kOutput, calls=%fused_computation.50 | convolution fusion | flops 4294967296 | bytes 14680064 | tf_op jit(solution)/shard_map/bxc,cd->bxd/dot_general | solution.py:57
  158.8 7.6 %fusion.32 = bf16[1,32,64,1024]{3,2,1,0:T(8,128)(2,1)S(1)} fusion(bf16[32,64,1024]{2,1,0:T(8,128)(2,1)S(1)} %copy-done.2, bf16[32,64,1024]{2,1,0:T(8,128)(2,1)S(1)} %copy-done.7, f32[32,64,1024]{2,1,0:T(8,128)} %fusion.33, f32[32,64,2048]{2,1,0:T(8,128)} %fusion.67, bf16[64,64,1]{1,0,2:T(8,128)(2,1)S(1)} %copy-done.16), kind=kOutput, calls=%fused_computation.49 | convolution fusion | flops 287309824 | bytes 33570816 | tf_op jit(solution)/shard_map/ux,bxc->buc/dot_general | solution.py:47
  168.8 98.6 %all_to_all.33 = bf16[1,32,64,1024]{3,1,0,2:T(8,128)(2,1)S(1)} all-to-all(bf16[1,32,64,1024]{3,1,0,2:T(8,128)(2,1)S(1)} %copy.12), channel_id=1, replica_groups=mesh['kpt'=2,'orb'=16] {'orb'}, dimensions={2} | all-to-all | bytes 8388608 | tf_op jit(solution)/shard_map/all_to_all | solution.py:76
  278.7 112.0 %all-reduce.2.cloned.1.call-done = f32[512,512]{1,0:T(8,128)} async-done(((f32[512,512]{1,0:T(8,128)}), f32[512,512]{1,0:T(8,128)}) %all-reduce.2.cloned.1.call-update) | async-done | bytes 1048592 | tf_op jit(solution)/shard_map/psum | solution.py:86
  436.7 4.6 multiply_reduce_fusion
  441.4 7.9 %reshape.13 = bf16[1,512,4,1024]{3,2,1,0:T(4,128)(2,1)} reshape(bf16[512,4096]{1,0:T(8,128)(2,1)} %get-tuple-element.3) | data formatting | bytes 8388608 | tf_op jit(solution)/shard_map/reshape | solution.py:99
  449.2 5.8 %all-to-all-start.1 = ((bf16[1,512,4,1024]{3,2,0,1:T(4,128)(2,1)}), bf16[1,512,4,1024]{3,2,0,1:T(4,128)(2,1)}, u32[]{:S(2)}, u32[]{:S(2)}) async-start(bf16[1,512,4,1024]{3,2,0,1:T(4,128)(2,1)} %bitcast.141), calls=%async_computation.1 | async-start | bytes 8388608 | tf_op jit(solution)/shard_map/all_to_all | solution.py:100
  459.0 88.2 %all-to-all-done.1 = bf16[1,512,4,1024]{3,2,0,1:T(4,128)(2,1)} async-done(((bf16[1,512,4,1024]{3,2,0,1:T(4,128)(2,1)}), bf16[1,512,4,1024]{3,2,0,1:T(4,128)(2,1)}, u32[]{:S(2)}, u32[]{:S(2)}) %all-to-all-start.1) | async-done | bytes 4194336 | tf_op jit(solution)/shard_map/all_to_all | solution.py:100
  547.2 6.4 %copy.15 = bf16[1,32,16,4,1024]{4,3,2,1,0:T(4,128)(2,1)} copy(bf16[1,32,16,4,1024]{4,3,1,2,0:T(4,128)(2,1)} %bitcast.24) | data formatting | bytes 8388608 | tf_op jit(solution)/shard_map/all_to_all | solution.py:100
  553.6 6.9 %all_to_all.30 = bf16[1,32,64,1024]{3,2,1,0:T(8,128)(2,1)} reshape(bf16[1,32,16,4,1024]{4,3,2,1,0:T(4,128)(2,1)} %copy.15) | data formatting | bytes 8388608 | tf_op jit(solution)/shard_map/all_to_all | solution.py:100
  (71 shorter events, 68.8 us)
Async XLA Ops:
  7.2 15.2 %copy-start.14 = (bf16[64,64,1]{1,0,2:T(8,128)(2,1)S(1)}, bf16[64,64,1]{1,0,2:T(8,128)(2,1)}, u32[]{:S(2)}) copy-start(bf16[64,64,1]{1,0,2:T(8,128)(2,1)} %constant.50) | copy-start | bytes 24580
  7.2 15.2 %copy-start.15 = (bf16[64,64,1]{1,0,2:T(8,128)(2,1)S(1)}, bf16[64,64,1]{1,0,2:T(8,128)(2,1)}, u32[]{:S(2)}) copy-start(bf16[64,64,1]{1,0,2:T(8,128)(2,1)} %constant.49) | copy-start | bytes 24580
  7.2 15.2 %copy-start.10 = (f32[64,1024]{1,0:T(8,128)S(1)}, f32[64,1024]{1,0:T(8,128)}, u32[]{:S(2)}) copy-start(f32[64,1024]{1,0:T(8,128)} %param.8) | copy-start | bytes 786436
  7.2 383.4 %all-reduce.2.cloned.1.call-start = ((), (), s32[]{:S(2)}) async-start(), calls=%async_computation.2 | async-start | bytes 2097152 | tf_op jit(solution)/shard_map/psum | solution.py:86
  30.1 7.1 %copy-start.8 = (bf16[1,32,64,1024]{3,2,1,0:T(8,128)(2,1)S(1)}, bf16[1,32,64,1024]{3,2,1,0:T(8,128)(2,1)}, u32[]{:S(2)}) copy-start(bf16[1,32,64,1024]{3,2,1,0:T(8,128)(2,1)} %param.7) | copy-start | bytes 12582916
  30.1 7.1 %copy-start.16 = (bf16[64,64,1]{1,0,2:T(8,128)(2,1)S(1)}, bf16[64,64,1]{1,0,2:T(8,128)(2,1)}, u32[]{:S(2)}) copy-start(bf16[64,64,1]{1,0,2:T(8,128)(2,1)} %constant.47) | copy-start | bytes 24580
  42.6 2.0 copy-start.3
  66.7 10.8 %copy-start.4 = (bf16[32,64,1024]{2,1,0:T(8,128)(2,1)S(1)}, bf16[32,64,1024]{2,1,0:T(8,128)(2,1)}, u32[]{:S(2)}) copy-start(bf16[32,64,1024]{2,1,0:T(8,128)(2,1)} %copy-done.3) | copy-start | bytes 12582916
  66.7 10.8 %copy-start.9 = (bf16[1,32,64,1024]{3,2,1,0:T(8,128)(2,1)S(1)}, bf16[1,32,64,1024]{3,2,1,0:T(8,128)(2,1)}, u32[]{:S(2)}) copy-start(bf16[1,32,64,1024]{3,2,1,0:T(8,128)(2,1)} %param.7) | copy-start | bytes 12582916
  85.1 2.0 copy-start
  101.1 7.8 %copy-start.17 = (bf16[1024,1024,1]{1,0,2:T(8,128)(2,1)S(1)}, bf16[1024,1024,1]{1,0,2:T(8,128)(2,1)}, u32[]{:S(2)}) copy-start(bf16[1024,1024,1]{1,0,2:T(8,128)(2,1)} %constant.51) | copy-start | bytes 6291460
  108.9 9.2 %copy-start.1 = (bf16[32,64,1024]{2,1,0:T(8,128)(2,1)S(1)}, bf16[32,64,1024]{2,1,0:T(8,128)(2,1)}, u32[]{:S(2)}) copy-start(bf16[32,64,1024]{2,1,0:T(8,128)(2,1)} %copy-done) | copy-start | bytes 12582916
  108.9 9.2 %copy-start.5 = (bf16[32,64,1024]{2,1,0:T(8,128)(2,1)S(1)}, bf16[32,64,1024]{2,1,0:T(8,128)(2,1)}, u32[]{:S(2)}) copy-start(bf16[32,64,1024]{2,1,0:T(8,128)(2,1)} %copy-done.3) | copy-start | bytes 12582916
  125.7 2.0 copy-start.6
  141.8 7.8 %copy-start.18 = (bf16[1024,1024,1]{1,0,2:T(8,128)(2,1)S(1)}, bf16[1024,1024,1]{1,0,2:T(8,128)(2,1)}, u32[]{:S(2)}) copy-start(bf16[1024,1024,1]{1,0,2:T(8,128)(2,1)} %constant.51) | copy-start | bytes 6291460
  149.6 9.2 %copy-start.2 = (bf16[32,64,1024]{2,1,0:T(8,128)(2,1)S(1)}, bf16[32,64,1024]{2,1,0:T(8,128)(2,1)}, u32[]{:S(2)}) copy-start(bf16[32,64,1024]{2,1,0:T(8,128)(2,1)} %copy-done) | copy-start | bytes 12582916
  149.6 9.2 %copy-start.7 = (bf16[32,64,1024]{2,1,0:T(8,128)(2,1)S(1)}, bf16[32,64,1024]{2,1,0:T(8,128)(2,1)}, u32[]{:S(2)}) copy-start(bf16[32,64,1024]{2,1,0:T(8,128)(2,1)} %copy-done.6) | copy-start | bytes 12582916
  273.3 2.0 copy-start.11
  390.6 6.2 %copy-start.13 = (f32[512,512]{1,0:T(8,128)S(1)}, f32[512,512]{1,0:T(8,128)}, u32[]{:S(2)}) copy-start(f32[512,512]{1,0:T(8,128)} %all-reduce.2.cloned.1.call-done) | copy-start | bytes 3145732
  433.0 3.7 copy-start.12
  449.2 97.9 %all-to-all-start.1 = ((bf16[1,512,4,1024]{3,2,0,1:T(4,128)(2,1)}), bf16[1,512,4,1024]{3,2,0,1:T(4,128)(2,1)}, u32[]{:S(2)}, u32[]{:S(2)}) async-start(bf16[1,512,4,1024]{3,2,0,1:T(4,128)(2,1)} %bitcast.141), calls=%async_computation.1 | async-start | bytes 8388608 | tf_op jit(solution)/shard_map/all_to_all | solution.py:100
Sparse Core Ops, SparseCore 0:
  278.8 111.7 all-reduce.1
where the time goes:
time: 575 us; the launch traced here: 567 us
  matrix products  204 us (35%)
  waiting for transfers between devices  200 us (35%)
  blocking collectives  103 us (18%)
  local copies, waits for them, and re-layouts  37.4 us (7%)
  between operations  15.3 us (3%)
  starting transfers between devices  5.82 us (1%)
    psum x1, waiting for transfers between devices, shards(): margin = lax.psum(partial_margin, 'orb')  112 us
    all_to_all x1, blocking collectives, shards(): lax.all_to_all(filtered, 'orb', split_axis=2, concat_axis=1, tiled=True)  98.6 us
    all_to_all x1, waiting for transfers between devices, shards(): lax.all_to_all(rotated_cells, 'orb', split_axis=1, concat_axis=2, tiled=T...  88.2 us
    dot_general x4, matrix products, hamiltonian(): jnp.einsum('bxc,cd->bxd', block, yz_table, preferred_element_type=jnp.flo...  57.7 us
    dot_general x4, matrix products, hamiltonian(): jnp.einsum('bxc,cd->bxd', back, mag_yz, preferred_element_type=jnp.float32)  36.2 us
    dot_general x4, matrix products, hamiltonian(): jnp.einsum('ux,bxc->buc', mag_xt, weighted, preferred_element_type=jnp.fl...  31 us
    dot_general x4, matrix products, hamiltonian(): jnp.einsum('ux,bxc->buc', kin_x, block, preferred_element_type=jnp.float32)  28.2 us
    dot_general x8, matrix products, shards(): factor = 0.5 * (3.0 * eye - jnp.dot(iterate_z, iterate_a, precision=hp))  15.5 us
  transfers between devices with their start and end apart: 2, of which 2 were waited for; matrix products, arithmetic and copies ran while one was open for 0% of the time, Pallas kernels for 0%

commit v1 on v0

--- a/solution.py
+++ b/solution.py
@@ -83,7 +83,7 @@
         lax.dot_general(flat, flat, (((1,), (1,)), ((), ())), preferred_element_type=jnp.float32)
         * inverse_cells
     )
-    margin = lax.psum(partial_margin, "orb")
+    margin = jax.lax.all_gather(partial_margin, "orb").sum(axis=0)
     scale = jnp.sqrt(jnp.sum(margin * margin) + margin_eps)
     eye = jnp.eye(count_orb, dtype=jnp.float32)
     iterate_a = margin / scale

time: 575 us -> 660 us (1.15)
  waiting for transfers between devices: 200 us -> 278 us
    all_gather x0 -> x1, waiting for transfers between devices: none -> 188 us  [shards(): margin = jax.lax.all_gather(partial_margin, 'orb').sum(axis=0)]
    psum x1 -> x0, waiting for transfers between devices: 112 us -> none  [shards(): margin = lax.psum(partial_margin, 'orb')]
    reduce_sum x0 -> x1, other arithmetic: none -> 7.91 us  [shards(): margin = jax.lax.all_gather(partial_margin, 'orb').sum(axis=0)]
where the time goes in v1:
time: 660 us; the launch traced here: 652 us
  waiting for transfers between devices  278 us (42%)
  matrix products  203 us (31%)
  blocking collectives  103 us (16%)
  local copies, waits for them, and re-layouts  37.4 us (6%)
  between operations  15.3 us (2%)
  other arithmetic  8.79 us (1%)
  starting transfers between devices  7.63 us (1%)
    all_gather x1, waiting for transfers between devices, shards(): margin = jax.lax.all_gather(partial_margin, 'orb').sum(axis=0)  188 us
    all_to_all x1, blocking collectives, shards(): lax.all_to_all(filtered, 'orb', split_axis=2, concat_axis=1, tiled=True)  98.6 us
    all_to_all x1, waiting for transfers between devices, shards(): lax.all_to_all(rotated_cells, 'orb', split_axis=1, concat_axis=2, tiled=T...  89.4 us
    dot_general x4, matrix products, hamiltonian(): jnp.einsum('bxc,cd->bxd', block, yz_table, preferred_element_type=jnp.flo...  58 us
    dot_general x4, matrix products, hamiltonian(): jnp.einsum('bxc,cd->bxd', back, mag_yz, preferred_element_type=jnp.float32)  36 us
    dot_general x4, matrix products, hamiltonian(): jnp.einsum('ux,bxc->buc', mag_xt, weighted, preferred_element_type=jnp.fl...  31 us
    dot_general x4, matrix products, hamiltonian(): jnp.einsum('ux,bxc->buc', kin_x, block, preferred_element_type=jnp.float32)  28.3 us
    dot_general x8, matrix products, shards(): factor = 0.5 * (3.0 * eye - jnp.dot(iterate_z, iterate_a, precision=hp))  14.5 us
  transfers between devices with their start and end apart: 2, of which 2 were waited for; matrix products, arithmetic and copies ran while one was open for 0% of the time, Pallas kernels for 0%

profile of v1, /device:TPU:14, one launch (start us, length us, event | category | flops | bytes accessed | tf_op | source)
XLA Modules:
  0.0 652.4 jit_solution(12365948020558679456)
XLA Ops:
  7.2 15.1 %convolution_bitcast_fusion = f32[32,64,2048]{2,1,0:T(8,128)} fusion(bf16[1024,2048,1]{1,0,2:T(8,128)(2,1)} %constant.48, bf16[1,32,64,1024]{3,2,1,0:T(8,128)(2,1)} %param.7), kind=kOutput, calls=%fused_computation.39 | convolution fusion | flops 8589934592 | bytes 25165824 | tf_op jit(solution)/shard_map/bxc,cd->bxd/dot_general | solution.py:44
  22.4 7.7 %fusion.20 = bf16[32,1024,64]{1,2,0:T(8,128)(2,1)} fusion(bf16[64,64,1]{1,0,2:T(8,128)(2,1)S(1)} %copy-done.13, f32[64,1024]{1,0:T(8,128)S(1)} %copy-done.10, bf16[64,64,1]{1,0,2:T(8,128)(2,1)S(1)} %copy-done.14, f32[32,64,2048]{2,1,0:T(8,128)} %convolution_bitcast_fusion), kind=kOutput, calls=%fused_computation.41 | convolution fusion | flops 541065216 | bytes 8667136 | tf_op jit(solution)/shard_map/ux,bxc->buc/dot_general | solution.py:54
  30.1 7.1 %fusion.39 = f32[32,64,1024]{2,1,0:T(8,128)S(1)} fusion(bf16[1024,1024,1]{1,0,2:T(8,128)(2,1)} %constant.51, bf16[32,1024,64]{1,2,0:T(8,128)(2,1)} %fusion.20), kind=kOutput, calls=%fused_computation.56 | convolution fusion | flops 4294967296 | bytes 14680064 | tf_op jit(solution)/shard_map/bxc,cd->bxd/dot_general | solution.py:57
  37.2 5.4 fusion.2
  44.6 14.6 %fusion.65 = f32[32,64,2048]{2,1,0:T(8,128)} fusion(bf16[32,64,1024]{2,1,0:T(8,128)(2,1)S(1)} %fusion.2, bf16[1024,2048,1]{1,0,2:T(8,128)(2,1)} %constant.48), kind=kOutput, calls=%fused_computation.94 | convolution fusion | flops 8589934592 | bytes 25165824 | tf_op jit(solution)/shard_map/bxc,cd->bxd/dot_general | solution.py:44
  59.2 7.7 %fusion.22 = bf16[32,1024,64]{1,2,0:T(8,128)(2,1)} fusion(bf16[64,64,1]{1,0,2:T(8,128)(2,1)S(1)} %copy-done.13, f32[64,1024]{1,0:T(8,128)S(1)} %copy-done.10, bf16[64,64,1]{1,0,2:T(8,128)(2,1)S(1)} %copy-done.14, f32[32,64,2048]{2,1,0:T(8,128)} %fusion.65), kind=kOutput, calls=%fused_computation.42 | convolution fusion | flops 541065216 | bytes 8667136 | tf_op jit(solution)/shard_map/ux,bxc->buc/dot_general | solution.py:54
  66.8 10.7 %fusion.37 = f32[32,64,1024]{2,1,0:T(8,128)} fusion(bf16[1024,1024,1]{1,0,2:T(8,128)(2,1)} %constant.51, bf16[32,1024,64]{1,2,0:T(8,128)(2,1)} %fusion.22), kind=kOutput, calls=%fused_computation.54 | convolution fusion | flops 4294967296 | bytes 14680064 | tf_op jit(solution)/shard_map/bxc,cd->bxd/dot_general | solution.py:57
  77.6 7.6 %fusion.3 = bf16[32,64,1024]{2,1,0:T(8,128)(2,1)S(1)} fusion(bf16[32,64,1024]{2,1,0:T(8,128)(2,1)S(1)} %copy-done.4, f32[32,64,1024]{2,1,0:T(8,128)} %fusion.37, f32[32,64,2048]{2,1,0:T(8,128)} %fusion.65, bf16[1,32,64,1024]{3,2,1,0:T(8,128)(2,1)S(1)} %copy-done.9, bf16[64,64,1]{1,0,2:T(8,128)(2,1)S(1)} %copy-done.15), kind=kOutput, calls=%fused_computation.9 | convolution fusion | flops 287309824 | bytes 33570816 | tf_op jit(solution)/shard_map/ux,bxc->buc/dot_general | solution.py:47
  87.2 14.1 %fusion.66 = f32[32,64,2048]{2,1,0:T(8,128)} fusion(bf16[32,64,1024]{2,1,0:T(8,128)(2,1)S(1)} %fusion.3, bf16[1024,2048,1]{1,0,2:T(8,128)(2,1)} %constant.48), kind=kOutput, calls=%fused_computation.95 | convolution fusion | flops 8589934592 | bytes 25165824 | tf_op jit(solution)/shard_map/bxc,cd->bxd/dot_general | solution.py:44
  101.3 7.8 %fusion.24 = bf16[32,1024,64]{1,2,0:T(8,128)(2,1)} fusion(bf16[64,64,1]{1,0,2:T(8,128)(2,1)S(1)} %copy-done.13, f32[64,1024]{1,0:T(8,128)S(1)} %copy-done.10, bf16[64,64,1]{1,0,2:T(8,128)(2,1)S(1)} %copy-done.14, f32[32,64,2048]{2,1,0:T(8,128)} %fusion.66), kind=kOutput, calls=%fused_computation.43 | convolution fusion | flops 541065216 | bytes 8667136 | tf_op jit(solution)/shard_map/ux,bxc->buc/dot_general | solution.py:54
  109.1 9.1 %fusion.35 = f32[32,64,1024]{2,1,0:T(8,128)} fusion(bf16[1024,1024,1]{1,0,2:T(8,128)(2,1)S(1)} %copy-done.16, bf16[32,1024,64]{1,2,0:T(8,128)(2,1)} %fusion.24), kind=kOutput, calls=%fused_computation.52 | convolution fusion | flops 4294967296 | bytes 14680064 | tf_op jit(solution)/shard_map/bxc,cd->bxd/dot_general | solution.py:57
  118.2 7.6 %fusion.6 = bf16[32,64,1024]{2,1,0:T(8,128)(2,1)S(1)} fusion(bf16[32,64,1024]{2,1,0:T(8,128)(2,1)S(1)} %copy-done.5, bf16[32,64,1024]{2,1,0:T(8,128)(2,1)S(1)} %copy-done.1, f32[32,64,1024]{2,1,0:T(8,128)} %fusion.35, f32[32,64,2048]{2,1,0:T(8,128)} %fusion.66, bf16[64,64,1]{1,0,2:T(8,128)(2,1)S(1)} %copy-done.15), kind=kOutput, calls=%fused_computation.12 | convolution fusion | flops 287309824 | bytes 33570816 | tf_op jit(solution)/shard_map/ux,bxc->buc/dot_general | solution.py:47
  127.9 14.2 %fusion.67 = f32[32,64,2048]{2,1,0:T(8,128)} fusion(bf16[32,64,1024]{2,1,0:T(8,128)(2,1)S(1)} %fusion.6, bf16[1024,2048,1]{1,0,2:T(8,128)(2,1)} %constant.48), kind=kOutput, calls=%fused_computation.96 | convolution fusion | flops 8589934592 | bytes 25165824 | tf_op jit(solution)/shard_map/bxc,cd->bxd/dot_general | solution.py:44
  142.0 7.8 %fusion.26 = bf16[32,1024,64]{1,2,0:T(8,128)(2,1)} fusion(bf16[64,64,1]{1,0,2:T(8,128)(2,1)S(1)} %copy-done.13, f32[64,1024]{1,0:T(8,128)S(1)} %copy-done.10, bf16[64,64,1]{1,0,2:T(8,128)(2,1)S(1)} %copy-done.14, f32[32,64,2048]{2,1,0:T(8,128)} %fusion.67), kind=kOutput, calls=%fused_computation.44 | convolution fusion | flops 541065216 | bytes 8667136 | tf_op jit(solution)/shard_map/ux,bxc->buc/dot_general | solution.py:54
  149.8 9.1 %fusion.33 = f32[32,64,1024]{2,1,0:T(8,128)} fusion(bf16[1024,1024,1]{1,0,2:T(8,128)(2,1)S(1)} %copy-done.17, bf16[32,1024,64]{1,2,0:T(8,128)(2,1)} %fusion.26), kind=kOutput, calls=%fused_computation.50 | convolution fusion | flops 4294967296 | bytes 14680064 | tf_op jit(solution)/shard_map/bxc,cd->bxd/dot_general | solution.py:57
  158.9 7.6 %fusion.32 = bf16[1,32,64,1024]{3,2,1,0:T(8,128)(2,1)S(1)} fusion(bf16[32,64,1024]{2,1,0:T(8,128)(2,1)S(1)} %copy-done.2, bf16[32,64,1024]{2,1,0:T(8,128)(2,1)S(1)} %copy-done.7, f32[32,64,1024]{2,1,0:T(8,128)} %fusion.33, f32[32,64,2048]{2,1,0:T(8,128)} %fusion.67, bf16[64,64,1]{1,0,2:T(8,128)(2,1)S(1)} %copy-done.15), kind=kOutput, calls=%fused_computation.49 | convolution fusion | flops 287309824 | bytes 33570816 | tf_op jit(solution)/shard_map/ux,bxc->buc/dot_general | solution.py:47
  168.9 98.6 %all_to_all.33 = bf16[1,32,64,1024]{3,1,0,2:T(8,128)(2,1)S(1)} all-to-all(bf16[1,32,64,1024]{3,1,0,2:T(8,128)(2,1)S(1)} %copy.16), channel_id=1, replica_groups=mesh['kpt'=2,'orb'=16] {'orb'}, dimensions={2} | all-to-all | bytes 8388608 | tf_op jit(solution)/shard_map/all_to_all | solution.py:76
  278.8 188.4 %all-gather.3.cloned.1.call-done = f32[8192,512]{1,0:T(8,128)} async-done(((f32[512,512]{1,0:T(8,128)}), f32[8192,512]{1,0:T(8,128)}) %all-gather.3.cloned.1.call-update) | async-done | bytes 16777232 | tf_op jit(solution)/shard_map/all_gather | solution.py:86
  467.1 7.9 %reduce_sum.27 = f32[512,512]{1,0:T(8,128)S(1)} reduce(f32[16,512,512]{2,1,0:T(8,128)} %bitcast.142, f32[]{:T(128)} %constant.28.clone.1), dimensions={0}, to_apply=%region_0.0 | reduce | flops 3932160 | bytes 17825796 | tf_op jit(solution)/shard_map/reduce_sum | solution.py:86
  523.2 7.9 %reshape.13 = bf16[1,512,4,1024]{3,2,1,0:T(4,128)(2,1)} reshape(bf16[512,4096]{1,0:T(8,128)(2,1)} %get-tuple-element.3) | data formatting | bytes 8388608 | tf_op jit(solution)/shard_map/reshape | solution.py:99
  531.1 7.6 %all-to-all-start.1 = ((bf16[1,512,4,1024]{3,2,0,1:T(4,128)(2,1)}), bf16[1,512,4,1024]{3,2,0,1:T(4,128)(2,1)}, u32[]{:S(2)}, u32[]{:S(2)}) async-start(bf16[1,512,4,1024]{3,2,0,1:T(4,128)(2,1)} %bitcast.143), calls=%async_computation.1 | async-start | bytes 8388608 | tf_op jit(solution)/shard_map/all_to_all | solution.py:100
  542.6 89.4 %all-to-all-done.1 = bf16[1,512,4,1024]{3,2,0,1:T(4,128)(2,1)} async-done(((bf16[1,512,4,1024]{3,2,0,1:T(4,128)(2,1)}), bf16[1,512,4,1024]{3,2,0,1:T(4,128)(2,1)}, u32[]{:S(2)}, u32[]{:S(2)}) %all-to-all-start.1) | async-done | bytes 4194336 | tf_op jit(solution)/shard_map/all_to_all | solution.py:100
  632.1 6.4 copy.19
  638.5 6.9 %all_to_all.30 = bf16[1,32,64,1024]{3,2,1,0:T(8,128)(2,1)} reshape(bf16[1,32,16,4,1024]{4,3,2,1,0:T(4,128)(2,1)} %copy.19) | data formatting | bytes 8388608 | tf_op jit(solution)/shard_map/all_to_all | solution.py:100
  (70 shorter events, 70.8 us)
Async XLA Ops:
  7.2 15.2 %copy-start.13 = (bf16[64,64,1]{1,0,2:T(8,128)(2,1)S(1)}, bf16[64,64,1]{1,0,2:T(8,128)(2,1)}, u32[]{:S(2)}) copy-start(bf16[64,64,1]{1,0,2:T(8,128)(2,1)} %constant.50) | copy-start | bytes 24580
  7.2 15.2 %copy-start.14 = (bf16[64,64,1]{1,0,2:T(8,128)(2,1)S(1)}, bf16[64,64,1]{1,0,2:T(8,128)(2,1)}, u32[]{:S(2)}) copy-start(bf16[64,64,1]{1,0,2:T(8,128)(2,1)} %constant.49) | copy-start | bytes 24580
  7.2 15.2 %copy-start.10 = (f32[64,1024]{1,0:T(8,128)S(1)}, f32[64,1024]{1,0:T(8,128)}, u32[]{:S(2)}) copy-start(f32[64,1024]{1,0:T(8,128)} %param.8) | copy-start | bytes 786436
  7.2 459.9 %all-gather.3.cloned.1.call-start = ((), (), s32[]{:S(2)}) async-start(), calls=%async_computation.2 | async-start | bytes 17825792 | tf_op jit(solution)/shard_map/all_gather | solution.py:86
  30.1 7.1 %copy-start.8 = (bf16[1,32,64,1024]{3,2,1,0:T(8,128)(2,1)S(1)}, bf16[1,32,64,1024]{3,2,1,0:T(8,128)(2,1)}, u32[]{:S(2)}) copy-start(bf16[1,32,64,1024]{3,2,1,0:T(8,128)(2,1)} %param.7) | copy-start | bytes 12582916
  30.1 7.1 %copy-start.15 = (bf16[64,64,1]{1,0,2:T(8,128)(2,1)S(1)}, bf16[64,64,1]{1,0,2:T(8,128)(2,1)}, u32[]{:S(2)}) copy-start(bf16[64,64,1]{1,0,2:T(8,128)(2,1)} %constant.47) | copy-start | bytes 24580
  42.6 2.0 copy-start.3
  66.8 10.8 %copy-start.4 = (bf16[32,64,1024]{2,1,0:T(8,128)(2,1)S(1)}, bf16[32,64,1024]{2,1,0:T(8,128)(2,1)}, u32[]{:S(2)}) copy-start(bf16[32,64,1024]{2,1,0:T(8,128)(2,1)} %copy-done.3) | copy-start | bytes 12582916
  66.8 10.8 %copy-start.9 = (bf16[1,32,64,1024]{3,2,1,0:T(8,128)(2,1)S(1)}, bf16[1,32,64,1024]{3,2,1,0:T(8,128)(2,1)}, u32[]{:S(2)}) copy-start(bf16[1,32,64,1024]{3,2,1,0:T(8,128)(2,1)} %param.7) | copy-start | bytes 12582916
  85.2 2.0 copy-start
  101.3 7.8 %copy-start.16 = (bf16[1024,1024,1]{1,0,2:T(8,128)(2,1)S(1)}, bf16[1024,1024,1]{1,0,2:T(8,128)(2,1)}, u32[]{:S(2)}) copy-start(bf16[1024,1024,1]{1,0,2:T(8,128)(2,1)} %constant.51) | copy-start | bytes 6291460
  109.1 9.1 %copy-start.1 = (bf16[32,64,1024]{2,1,0:T(8,128)(2,1)S(1)}, bf16[32,64,1024]{2,1,0:T(8,128)(2,1)}, u32[]{:S(2)}) copy-start(bf16[32,64,1024]{2,1,0:T(8,128)(2,1)} %copy-done) | copy-start | bytes 12582916
  109.1 9.1 %copy-start.5 = (bf16[32,64,1024]{2,1,0:T(8,128)(2,1)S(1)}, bf16[32,64,1024]{2,1,0:T(8,128)(2,1)}, u32[]{:S(2)}) copy-start(bf16[32,64,1024]{2,1,0:T(8,128)(2,1)} %copy-done.3) | copy-start | bytes 12582916
  125.8 2.0 copy-start.6
  142.0 7.8 %copy-start.17 = (bf16[1024,1024,1]{1,0,2:T(8,128)(2,1)S(1)}, bf16[1024,1024,1]{1,0,2:T(8,128)(2,1)}, u32[]{:S(2)}) copy-start(bf16[1024,1024,1]{1,0,2:T(8,128)(2,1)} %constant.51) | copy-start | bytes 6291460
  149.8 9.1 %copy-start.2 = (bf16[32,64,1024]{2,1,0:T(8,128)(2,1)S(1)}, bf16[32,64,1024]{2,1,0:T(8,128)(2,1)}, u32[]{:S(2)}) copy-start(bf16[32,64,1024]{2,1,0:T(8,128)(2,1)} %copy-done) | copy-start | bytes 12582916
  149.8 9.1 %copy-start.7 = (bf16[32,64,1024]{2,1,0:T(8,128)(2,1)S(1)}, bf16[32,64,1024]{2,1,0:T(8,128)(2,1)}, u32[]{:S(2)}) copy-start(bf16[32,64,1024]{2,1,0:T(8,128)(2,1)} %copy-done.6) | copy-start | bytes 12582916
  273.4 2.0 copy-start.11
  514.9 3.9 copy-start.12
  531.1 101.0 %all-to-all-start.1 = ((bf16[1,512,4,1024]{3,2,0,1:T(4,128)(2,1)}), bf16[1,512,4,1024]{3,2,0,1:T(4,128)(2,1)}, u32[]{:S(2)}, u32[]{:S(2)}) async-start(bf16[1,512,4,1024]{3,2,0,1:T(4,128)(2,1)} %bitcast.143), calls=%async_computation.1 | async-start | bytes 8388608 | tf_op jit(solution)/shard_map/all_to_all | solution.py:100
Sparse Core Ops, SparseCore 0:
  278.9 188.1 all-gather.2
